TPU v7x, 32 devices: a whole 2x2x4 slice. The times are simulated.
32 devices in a mesh: grp: 2 (over y), az: 4 (over z), el: 2 (over x), fq: 2 (over core).
Axes of the slice: x: 2, y: 2, z: 4, core: 2. Of those that a mesh axis runs over, the one named last changes fastest.
Arguments:
- polar: bfloat16 [2, 64, 1024, 768], P(None, ('grp', 'el'), 'az', 'fq'), parts along dimension 1, may hold values from -6 to 6
- band_offset: int32 [1024, 768], P('az', 'fq'), may hold values from -8 to 5, as said below
- tap_count: int32 [1024, 768], P('az', 'fq'), may hold values from 4 to 8
- tap_weight: bfloat16 [8, 1024, 768], P(None, 'az', 'fq'), may hold values from -2.390625 to 2.390625
Outputs:
- image_out: bfloat16 [2, 64, 768, 1024], P(None, ('grp', 'el'), ('az', 'fq')), parts along dimension 1
There are 2 independent parts, one for each index of `grp`. A program takes and returns all parts, laid end to end along the dimension named above; an argument that names none is the same for every part. Nothing has to cross between parts.
Inputs may be any that keep to these rules, and one draw needn't show every extreme that they name: band_offset[j, f] lies between -8 and 9 - tap_count[j, f], so a band reads azimuths j - 8 to j + 8; both ends are reached.
All inputs are finite; a program needn't handle non-finite values.
Results may differ from a plain program's by a relative error of at most 0.0074.
Values may be sent and summed in bfloat16 or wider, within the bound.
A program may use at most 128 MiB of HBM per device.

v0:
```python
import math

import jax
import jax.numpy as jnp
from jax import lax
from jax.experimental import pallas as pl
from jax.experimental.pallas import tpu as pltpu
from jax.sharding import PartitionSpec as P

F = 768
A = 1024
E = 32
HW = 8
KT = 8
LANES = 128
GROUP = 16
TAPS = 2 * HW + 1
BATCH = 4
LATE = 4
SLOTS = 4
FIRST = 2
SPLIT = 2
TILE = 256
MESH = pl.DeviceIdType.MESH


def with_halo(cells, sides, width):
    for axis, dim in sides:
        count = lax.axis_size(axis)
        ends = count - 1
        head = lax.slice_in_dim(cells, 0, width, axis=dim)
        tail = lax.slice_in_dim(cells, cells.shape[dim] - width, cells.shape[dim], axis=dim)
        cells = jnp.concatenate(
            [
                lax.ppermute(tail, axis, [(i, (i + 1) % count) for i in range(ends)]),
                cells,
                lax.ppermute(head, axis, [((i + 1) % count, i) for i in range(ends)]),
            ],
            axis=dim,
        )
    return cells


def table_pair(row_ids, col_ids, length):
    product = row_ids[:, None] * col_ids[None, :] % length
    angle = product.astype(jnp.float32) * (2.0 * math.pi / length)
    return (jnp.cos(angle).astype(jnp.bfloat16), jnp.sin(angle).astype(jnp.bfloat16))


def on_device(polar, band_offset, tap_count, tap_weight):
    shape_all = polar.shape
    col_count = shape_all[2]
    freq_count = shape_all[3]
    az_count = lax.axis_size("az")
    fq_count = lax.axis_size("fq")
    el_count = lax.axis_size("el")
    padded = with_halo(polar, (("az", 2),), HW)
    window = col_count + 2 * HW
    column = jnp.arange(col_count, dtype=jnp.int32)[:, None]
    position = jnp.arange(window, dtype=jnp.int32)[None, :, None]
    band_matrix = jnp.zeros((col_count, window, freq_count), jnp.bfloat16)
    for tap_index in range(KT):
        reach = column + HW + band_offset + tap_index
        matches = (position == reach[:, None, :]) & (tap_index < tap_count)[:, None, :]
        band_matrix = jnp.where(matches, tap_weight[tap_index][:, None, :], band_matrix)
    interpolated = jnp.einsum(
        "jaf,ceaf->cejf", band_matrix, padded, preferred_element_type=jnp.float32
    ).astype(jnp.bfloat16)
    fq_index = lax.axis_index("fq")
    bin_count = F // (fq_count * az_count)
    az_block = jnp.arange(az_count, dtype=jnp.int32)[:, None]
    bin_local = jnp.arange(bin_count, dtype=jnp.int32)[None, :]
    range_bins = ((az_block * fq_count + fq_index) * bin_count + bin_local).reshape(-1)
    cos_f, sin_f = table_pair(jnp.arange(F, dtype=jnp.int32), range_bins, F)
    shard_piece = lax.all_gather(interpolated, "fq", axis=3, tiled=True)
    cos_rows = cos_f
    sin_rows = sin_f
    real_part = jnp.einsum(
        "ejf,fk->ekj", shard_piece[0], cos_rows, preferred_element_type=jnp.float32
    ) - jnp.einsum("ejf,fk->ekj", shard_piece[1], sin_rows, preferred_element_type=jnp.float32)
    imag_part = jnp.einsum(
        "ejf,fk->ekj", shard_piece[0], sin_rows, preferred_element_type=jnp.float32
    ) + jnp.einsum("ejf,fk->ekj", shard_piece[1], cos_rows, preferred_element_type=jnp.float32)
    summed = jnp.stack([real_part, imag_part])
    ranged = (summed * (1.0 / math.sqrt(F))).astype(jnp.bfloat16)
    azim_ids = jnp.arange(A, dtype=jnp.int32)
    cos_a, sin_a = table_pair(azim_ids, azim_ids, A)
    block_data = lax.all_to_all(ranged, "az", split_axis=2, concat_axis=3, tiled=True)
    real_part = jnp.einsum(
        "ekj,jm->ekm", block_data[0], cos_a, preferred_element_type=jnp.float32
    ) - jnp.einsum("ekj,jm->ekm", block_data[1], sin_a, preferred_element_type=jnp.float32)
    imag_part = jnp.einsum(
        "ekj,jm->ekm", block_data[0], sin_a, preferred_element_type=jnp.float32
    ) + jnp.einsum("ekj,jm->ekm", block_data[1], cos_a, preferred_element_type=jnp.float32)
    crossed = (jnp.stack([real_part, imag_part]) * (1.0 / math.sqrt(A))).astype(jnp.bfloat16)
    elev_ids = jnp.arange(E, dtype=jnp.int32)
    el_index = lax.axis_index("el")
    height_count = E // el_count
    height_rows = el_index * height_count + jnp.arange(height_count, dtype=jnp.int32)
    cos_e, sin_e = table_pair(elev_ids, height_rows, E)
    shard_piece = lax.all_gather(crossed, "el", axis=1, tiled=True)
    cos_rows = cos_e
    sin_rows = sin_e
    real_part = jnp.einsum(
        "eh,ekm->hkm", cos_rows, shard_piece[0], preferred_element_type=jnp.float32
    ) - jnp.einsum("eh,ekm->hkm", sin_rows, shard_piece[1], preferred_element_type=jnp.float32)
    imag_part = jnp.einsum(
        "eh,ekm->hkm", sin_rows, shard_piece[0], preferred_element_type=jnp.float32
    ) + jnp.einsum("eh,ekm->hkm", cos_rows, shard_piece[1], preferred_element_type=jnp.float32)
    totals = jnp.stack([real_part, imag_part])
    image_out = (totals * (1.0 / math.sqrt(E))).astype(jnp.bfloat16)
    return image_out


def small_trig(product, length):
    value = product.astype(jnp.float32)
    turns = jnp.floor(value * (1.0 / length))
    angle = (value - turns * length) * (2.0 * math.pi / length)
    return jnp.cos(angle), jnp.sin(angle)


def iota(shape, dim):
    return lax.broadcasted_iota(jnp.int32, shape, dim)


def fused_body(
    polar, off_h, cnt_h, tap_h, out_h,
    xs, buf, pv, wt, offv, cntv, tapv, hl, hr,
    lowc, lows, highc, highs, rtab, cos_a, sin_a, htab,
    rl, zl, er, eh, ez, ch, ost, est,
    in_sem, pv_sem, halo_s, halo_r, fq_s, fq_r, zl_s, zl_r,
    xe_s, xe_r, ze_s, ze_r, xa_s, xa_r, xb_s, xb_r, lo_sem, eo_sem,
):
    n_az = lax.axis_size("az")
    az, fq, el = (lax.axis_index(name) for name in ("az", "fq", "el"))
    _, cuts, cols, freqs = polar.shape
    parts = freqs // LANES
    heights = E // 2
    late = LATE * GROUP
    bins = out_h.shape[2]
    early_groups = (bins - late) // GROUP
    batches = cuts // BATCH
    steps = cols // GROUP

    def at_az(shift):
        return {"az": lax.rem(az + shift, n_az)}

    def lane_block(index, size):
        return pl.ds(pl.multiple_of(index * size, LANES), size)

    fq_peer = {"fq": 1 - fq}
    el_peer = {"el": 1 - el}
    own_cols = lane_block(az, cols)

    def from_az(shift):
        return lane_block(lax.rem(az - shift + n_az, n_az), cols)

    def remote(source, target, send, recv, where):
        return pltpu.make_async_remote_copy(
            src_ref=source,
            dst_ref=target,
            send_sem=send,
            recv_sem=recv,
            device_id=where,
            device_id_type=MESH,
        )

    def polar_copy(c):
        slot = lax.rem(c, SLOTS)
        return pltpu.make_async_copy(polar.at[:, c], pv.at[slot], pv_sem.at[slot])

    spans = (pl.ds(0, FIRST), pl.ds(FIRST, cuts - FIRST))

    def halo_up(k):
        return remote(
            polar.at[:, spans[k], pl.ds(cols - HW, HW)],
            hl.at[:, spans[k]],
            halo_s.at[0, k],
            halo_r.at[0, k],
            at_az(1),
        )

    def halo_down(k):
        return remote(
            polar.at[:, spans[k], pl.ds(0, HW)],
            hr.at[:, spans[k]],
            halo_s.at[1, k],
            halo_r.at[1, k],
            at_az(n_az - 1),
        )

    def fq_copy(c, lanes):
        return remote(
            xs.at[c, :, :, lanes], xs.at[c, :, :, lanes], fq_s.at[c], fq_r.at[c], fq_peer
        )

    def zl_copy(c, shift, lanes):
        return remote(
            rl.at[c, shift - 1],
            zl.at[c // BATCH, :, lax.rem(c, BATCH), :, lanes],
            zl_s.at[c, shift - 1],
            zl_r.at[c, shift - 1],
            at_az(shift),
        )

    def xe_copy(c):
        return remote(
            er.at[:, :, 0, :, c], er.at[:, :, 1, :, c], xe_s.at[c], xe_r.at[c], el_peer
        )

    def ze_copy(g, q, shift, lanes):
        span = pl.ds(q * (heights // SPLIT), heights // SPLIT)
        return remote(
            eh.at[g, shift - 1, :, span],
            ez.at[g, :, span, :, lanes],
            ze_s.at[g, q, shift - 1],
            ze_r.at[g, q, shift - 1],
            at_az(shift),
        )

    def xa_copy(b):
        span = pl.ds(b * BATCH, BATCH)
        return remote(
            ch.at[:, 0, :, span], ch.at[:, 1, :, span], xa_s.at[b], xa_r.at[b], el_peer
        )

    def xb_copy(b, g):
        span = pl.ds(b * BATCH, BATCH)
        half = batches // 2
        return remote(
            ch.at[g, 0, :, span],
            ch.at[g, 1, :, span],
            xb_s.at[b - half, g],
            xb_r.at[b - half, g],
            el_peer,
        )

    barrier = pltpu.get_barrier_semaphore()
    peers = [fq_peer, el_peer] + [at_az(s) for s in range(1, n_az)]
    for peer in peers:
        pl.semaphore_signal(barrier, inc=1, device_id=peer, device_id_type=MESH)
    loads = [
        pltpu.make_async_copy(off_h, offv, in_sem.at[0]),
        pltpu.make_async_copy(cnt_h, cntv, in_sem.at[1]),
        pltpu.make_async_copy(tap_h, tapv, in_sem.at[2]),
    ]
    for load in loads:
        load.start()
    for c in range(SLOTS):
        polar_copy(c).start()

    @pl.when(az == 0)
    def _():
        hl[...] = jnp.zeros(hl.shape, hl.dtype)

    @pl.when(az == n_az - 1)
    def _():
        hr[...] = jnp.zeros(hr.shape, hr.dtype)

    pl.semaphore_wait(barrier, len(peers))

    @pl.when(az < n_az - 1)
    def _():
        for k in range(2):
            halo_up(k).start()

    @pl.when(az > 0)
    def _():
        for k in range(2):
            halo_down(k).start()

    block = 32
    blocks = n_az * bins // block
    per = bins // block
    row = iota((16, F), 0)
    shift = jnp.zeros((16, F), jnp.int32)
    for s in range(1, n_az):
        shift = shift + (row >= s * per).astype(jnp.int32)
    inner = row - shift * per
    target = az + shift
    target = jnp.where(target >= n_az, target - n_az, target)
    starts = (target * 2 + fq) * bins + inner * block
    wide = slice(0, F)
    highc[0:16, wide], highs[0:16, wide] = small_trig(starts * iota((16, F), 1), F)
    lowc[:, wide], lows[:, wide] = small_trig(iota((block, F), 0) * iota((block, F), 1), F)

    @pl.loop(0, blocks)
    def _(i):
        hc, hs = highc[pl.ds(i, 1), wide], highs[pl.ds(i, 1), wide]
        lc, ls = lowc[:, wide], lows[:, wide]
        at = pl.ds(pl.multiple_of(i * block, block), block)
        rtab[at, :] = (hc * lc - hs * ls).astype(jnp.bfloat16)
        at = pl.ds(pl.multiple_of((blocks + i) * block, block), block)
        rtab[at, :] = (hs * lc + hc * ls).astype(jnp.bfloat16)

    for load in loads:
        load.wait()

    @pl.loop(0, parts * steps)
    def _(i):
        g = i // steps
        rows = pl.ds(pl.multiple_of(lax.rem(i, steps) * GROUP, GROUP), GROUP)
        lanes = lane_block(g, LANES)
        rel = offv[rows, lanes] + HW
        cnt = cntv[rows, lanes]
        zero = jnp.zeros(rel.shape, jnp.float32)
        taps = [
            jnp.where(t < cnt, tapv[t, rows, lanes].astype(jnp.float32), zero)
            for t in range(KT)
        ]
        for bit in range(4):
            step = 1 << bit
            on = (rel & step) != 0
            size = min(TAPS, len(taps) + step)
            taps = [
                jnp.where(
                    on,
                    taps[d - step] if d >= step else zero,
                    taps[d] if d < len(taps) else zero,
                )
                for d in range(size)
            ]
        for d in range(TAPS):
            wt[d, g, rows, :] = taps[d]

    def wait_halo(k):
        @pl.when(az > 0)
        def _():
            halo_up(k).wait_recv()

        @pl.when(az < n_az - 1)
        def _():
            halo_down(k).wait_recv()

    def interpolate(c):
        slot = lax.rem(c, SLOTS)
        polar_copy(c).wait()

        @pl.when(c == 0)
        def _():
            wait_halo(0)

        @pl.when(c == FIRST)
        def _():
            wait_halo(1)

        for p in range(2):
            for g in range(parts):
                lanes = slice(g * LANES, (g + 1) * LANES)
                buf[p, g, 0:HW, :] = hl[p, c, :, lanes].astype(jnp.float32)
                buf[p, g, HW : HW + cols, :] = pv[slot, p, :, lanes].astype(jnp.float32)
                buf[p, g, HW + cols :, :] = hr[p, c, :, lanes].astype(jnp.float32)

        @pl.loop(0, parts * steps)
        def _(i):
            g = i // steps
            base = pl.multiple_of(lax.rem(i, steps) * GROUP, GROUP)
            lanes = lane_block(fq * parts + g, LANES)
            weights = [wt[d, g, pl.ds(base, GROUP), :] for d in range(TAPS)]
            for p in range(2):
                acc = [None, None]
                for o in range(TAPS + 8):
                    cell = buf[p, g, pl.ds(base + o, 8), :]
                    for v in range(2):
                        d = o - 8 * v
                        if 0 <= d < TAPS:
                            term = weights[d][8 * v : 8 * v + 8] * cell
                            acc[v] = term if acc[v] is None else acc[v] + term
                value = jnp.concatenate(acc, axis=0).astype(jnp.bfloat16)
                xs[c, p, pl.ds(base, GROUP), lanes] = value

        fq_copy(c, lane_block(fq, freqs)).start()

        @pl.when(c + SLOTS < cuts)
        def _():
            polar_copy(c + SLOTS).start()

    def range_step(c):
        fq_copy(c, lane_block(1 - fq, freqs)).wait_recv()
        dims = (((1,), (1,)), ((), ()))
        table = rtab[...]
        fr = lax.dot_general(table, xs[c, 0], dims, preferred_element_type=jnp.float32)
        fi = lax.dot_general(table, xs[c, 1], dims, preferred_element_type=jnp.float32)
        half = n_az * bins
        scale = 1.0 / math.sqrt(F)
        real = ((fr[:half] - fi[half:]) * scale).astype(jnp.bfloat16)
        imag = ((fr[half:] + fi[:half]) * scale).astype(jnp.bfloat16)
        b, k = c // BATCH, lax.rem(c, BATCH)
        for p, part in enumerate((real, imag)):
            for s in range(n_az):
                piece = part[s * bins : s * bins + late]
                if s == 0:
                    zl[b, p, k, :, own_cols] = piece
                else:
                    rl[c, s - 1, p] = piece
                for g in range(early_groups):
                    at = s * bins + late + g * GROUP
                    er[g, s, 0, p, c] = part[at : at + GROUP]
        for s in order:
            zl_copy(c, s, own_cols).start()
        xe_copy(c).start()

    middle = n_az // 2
    order = [middle] + [s for s in range(1, n_az) if s != middle]

    def azimuth_tables():
        size = 1024 // block
        col = iota((block, A), 1)
        lowc[...], lows[...] = small_trig(iota((block, A), 0) * col, A)
        highc[...], highs[...] = small_trig(iota((A // block, A), 0) * block * col, A)

        @pl.loop(0, A // block)
        def _(i):
            hc, hs = highc[pl.ds(i, 1), :], highs[pl.ds(i, 1), :]
            at = pl.ds(pl.multiple_of(i * block, block), block)
            cos_a[at, :] = (hc * lowc[...] - hs * lows[...]).astype(jnp.bfloat16)
            sin_a[at, :] = (hs * lowc[...] + hc * lows[...]).astype(jnp.bfloat16)

    def height_tables():
        rows, width = 2 * heights, 4 * cuts
        row, col = iota((rows, 128), 0), iota((rows, 128), 1)
        out_imag = row >= heights
        height = el * heights + jnp.where(out_imag, row - heights, row)
        other = col >= 2 * cuts
        inner = jnp.where(other, col - 2 * cuts, col)
        in_imag = inner >= cuts
        source = jnp.where(other, 1 - el, el)
        elev = source * cuts + jnp.where(in_imag, inner - cuts, inner)
        cos_e, sin_e = small_trig(height * elev, E)
        sign = jnp.where(out_imag, sin_e, -sin_e)
        small = jnp.where(out_imag == in_imag, cos_e, sign)
        small = jnp.where(col < width, small, 0.0).astype(jnp.bfloat16)
        tall = rows * GROUP
        take_row = (iota((tall, rows), 0) // GROUP == iota((tall, rows), 1)).astype(
            jnp.bfloat16
        )
        mid = jnp.dot(take_row, small, preferred_element_type=jnp.float32)
        mid = mid.astype(jnp.bfloat16)

        @pl.loop(0, width * GROUP // TILE)
        def _(i):
            shape = (128, TILE)
            col_at = iota(shape, 1) + i * TILE
            take_col = (iota(shape, 0) == col_at // GROUP).astype(jnp.bfloat16)
            spread = jnp.dot(mid, take_col, preferred_element_type=jnp.float32)
            shape = (tall, TILE)
            same = (iota(shape, 0) & (GROUP - 1)) == (iota(shape, 1) & (GROUP - 1))
            htab[:, lane_block(i, TILE)] = jnp.where(same, spread, 0.0).astype(jnp.bfloat16)

    def cross_tile(left, t):
        rows = left.shape[0] // 2
        scale = 1.0 / math.sqrt(A)
        by_cos = jnp.dot(left, cos_a[:, lane_block(t, TILE)], preferred_element_type=jnp.float32)
        by_sin = jnp.dot(left, sin_a[:, lane_block(t, TILE)], preferred_element_type=jnp.float32)
        real = ((by_cos[:rows] - by_sin[rows:]) * scale).astype(jnp.bfloat16)
        imag = ((by_sin[:rows] + by_cos[rows:]) * scale).astype(jnp.bfloat16)
        return real, imag

    def cross_late(b):
        for k in range(BATCH):
            for s in order:
                zl_copy(b * BATCH + k, s, from_az(s)).wait_recv()

        @pl.loop(0, A // TILE)
        def _(t):
            left = zl[b].reshape(2 * BATCH * late, A)
            for p, part in enumerate(cross_tile(left, t)):
                part = part.reshape(BATCH, LATE, GROUP, TILE)
                for g in range(LATE):
                    span = pl.ds(b * BATCH, BATCH)
                    ch[g, 0, p, span, :, lane_block(t, TILE)] = part[:, g]

    def early_heights(g):
        @pl.loop(0, n_az)
        def _(s):
            data = er[g, s].reshape(4 * cuts * GROUP, cols)
            total = jnp.dot(htab[...], data, preferred_element_type=jnp.float32)
            total = (total * (1.0 / math.sqrt(E))).astype(jnp.bfloat16)
            total = total.reshape(2, heights, GROUP, cols)

            @pl.when(s == 0)
            def _():
                ez[g, :, :, :, own_cols] = total

            @pl.when(s > 0)
            def _():
                eh[g, s - 1] = total

        for q in range(SPLIT):
            for s in order:
                ze_copy(g, q, s, own_cols).start()

    def early_out(g, q):
        span = pl.ds(q * (heights // SPLIT), heights // SPLIT)
        return pltpu.make_async_copy(
            est.at[g, q],
            out_h.at[:, span, pl.ds(late + g * GROUP, GROUP), :],
            eo_sem.at[g, q],
        )

    def cross_early(g, q):
        for s in order:
            ze_copy(g, q, s, from_az(s)).wait_recv()
        some = heights // SPLIT

        @pl.loop(0, A // TILE)
        def _(t):
            left = ez[g, :, q * some : (q + 1) * some].reshape(2 * some * GROUP, A)
            for p, part in enumerate(cross_tile(left, t)):
                est[g, q, p, :, :, lane_block(t, TILE)] = part.reshape(some, GROUP, TILE)

        early_out(g, q).start()

    def late_out(g):
        return pltpu.make_async_copy(
            ost.at[g % 2], out_h.at[:, :, pl.ds(g * GROUP, GROUP), :], lo_sem.at[g]
        )

    def late_heights(g):
        if g == 0:
            for b in range(batches // 2):
                xa_copy(b).wait_recv()
        for b in range(batches // 2, batches):
            xb_copy(b, g).wait_recv()
        if g >= 2:
            late_out(g - 2).wait()

        @pl.loop(0, A // TILE)
        def _(t):
            at = lane_block(t, TILE)
            data = ch[g, :, :, :, :, at].reshape(4 * cuts * GROUP, TILE)
            total = jnp.dot(htab[...], data, preferred_element_type=jnp.float32)
            total = (total * (1.0 / math.sqrt(E))).astype(jnp.bfloat16)
            ost[g % 2, :, :, :, at] = total.reshape(2, heights, GROUP, TILE)

        late_out(g).start()

    def front(first, last):
        @pl.loop(first, last)
        def _(c):
            @pl.when(c < cuts)
            def _():
                interpolate(c)

            @pl.when(c > 0)
            def _():
                range_step(c - 1)

    pause = cuts // 2 + 2
    front(0, pause)
    azimuth_tables()
    height_tables()
    cross_late(0)
    xa_copy(0).start()
    front(pause, cuts + 1)
    cross_late(1)
    xa_copy(1).start()
    cross_late(2)
    xb_copy(2, 0).start()
    xb_copy(2, 1).start()
    for c in range(cuts):
        xe_copy(c).wait_recv()
    for g in range(early_groups):
        early_heights(g)
    cross_late(3)
    for b, g in ((3, 0), (3, 1), (2, 2), (3, 2), (2, 3), (3, 3)):
        xb_copy(b, g).start()
    cross_early(0, 0)
    late_heights(0)
    cross_early(0, 1)
    late_heights(1)
    cross_early(1, 0)
    late_heights(2)
    cross_early(1, 1)
    late_heights(3)

    @pl.when(az < n_az - 1)
    def _():
        for k in range(2):
            halo_up(k).wait_send()

    @pl.when(az > 0)
    def _():
        for k in range(2):
            halo_down(k).wait_send()

    @pl.loop(0, cuts)
    def _(c):
        fq_copy(c, lane_block(fq, freqs)).wait_send()
        for s in order:
            zl_copy(c, s, own_cols).wait_send()
        xe_copy(c).wait_send()

    for g in range(early_groups):
        for q in range(SPLIT):
            for s in order:
                ze_copy(g, q, s, own_cols).wait_send()
    for b in range(batches // 2):
        xa_copy(b).wait_send()
    for b in range(batches // 2, batches):
        for g in range(LATE):
            xb_copy(b, g).wait_send()
    for g in range(early_groups):
        for q in range(SPLIT):
            early_out(g, q).wait()
    for g in range(LATE - 2, LATE):
        late_out(g).wait()


def fused(polar, band_offset, tap_count, tap_weight):
    _, cuts, cols, freqs = polar.shape
    n_az = lax.axis_size("az")
    bins = F // (2 * n_az)
    late = LATE * GROUP
    heights = E // 2
    parts = freqs // LANES
    groups = (bins - late) // GROUP
    batches = cuts // BATCH
    far = n_az - 1
    half = jnp.bfloat16
    vmem = pltpu.VMEM
    dma = pltpu.SemaphoreType.DMA
    return pl.pallas_call(
        fused_body,
        out_shape=jax.ShapeDtypeStruct((2, heights, bins, A), half),
        in_specs=[pl.BlockSpec(memory_space=pl.ANY)] * 4,
        out_specs=pl.BlockSpec(memory_space=pl.ANY),
        scratch_shapes=[
            vmem((cuts, 2, cols, F), half),
            vmem((2, parts, cols + 2 * HW, LANES), jnp.float32),
            vmem((SLOTS, 2, cols, freqs), half),
            vmem((TAPS, parts, cols, LANES), jnp.float32),
            vmem((cols, freqs), jnp.int32),
            vmem((cols, freqs), jnp.int32),
            vmem((KT, cols, freqs), half),
            vmem((2, cuts, HW, freqs), half),
            vmem((2, cuts, HW, freqs), half),
            vmem((32, A), jnp.float32),
            vmem((32, A), jnp.float32),
            vmem((32, A), jnp.float32),
            vmem((32, A), jnp.float32),
            vmem((2 * n_az * bins, F), half),
            vmem((A, A), half),
            vmem((A, A), half),
            vmem((2 * heights * GROUP, 4 * cuts * GROUP), half),
            vmem((cuts, far, 2, late, cols), half),
            vmem((batches, 2, BATCH, late, A), half),
            vmem((groups, n_az, 2, 2, cuts, GROUP, cols), half),
            vmem((groups, far, 2, heights, GROUP, cols), half),
            vmem((groups, 2, heights, GROUP, A), half),
            vmem((LATE, 2, 2, cuts, GROUP, A), half),
            vmem((2, 2, heights, GROUP, A), half),
            vmem((groups, SPLIT, 2, heights // SPLIT, GROUP, A), half),
            dma((3,)),
            dma((SLOTS,)),
            dma((2, 2)),
            dma((2, 2)),
            dma((cuts,)),
            dma((cuts,)),
            dma((cuts, far)),
            dma((cuts, far)),
            dma((cuts,)),
            dma((cuts,)),
            dma((groups, SPLIT, far)),
            dma((groups, SPLIT, far)),
            dma((batches // 2,)),
            dma((batches // 2,)),
            dma((batches // 2, LATE)),
            dma((batches // 2, LATE)),
            dma((LATE,)),
            dma((groups, SPLIT)),
        ],
        compiler_params=pltpu.CompilerParams(
            collective_id=0, has_side_effects=True, vmem_limit_bytes=67043328
        ),
        name="image",
    )(polar, band_offset, tap_count, tap_weight)


def pick(polar, band_offset, tap_count, tap_weight):
    _, e_here, col_count, freq_count = polar.shape
    az_count = lax.axis_size("az")
    bins = F // (lax.axis_size("fq") * az_count)
    fits = (
        lax.axis_size("fq") == 2
        and lax.axis_size("el") == 2
        and az_count == 4
        and e_here == 4 * BATCH
        and bins == (LATE + 2) * GROUP
        and col_count == TILE
        and freq_count % LANES == 0
    )
    run = fused if fits else on_device
    return run(polar, band_offset, tap_count, tap_weight)


def solution(mesh):
    in_specs = (
        P(None, ("grp", "el"), "az", "fq"),
        P("az", "fq"),
        P("az", "fq"),
        P(None, "az", "fq"),
    )
    out_specs = P(None, ("grp", "el"), ("az", "fq"), None)
    return jax.shard_map(
        pick, mesh=mesh, in_specs=in_specs, out_specs=out_specs, check_vma=False
    )
```

profile of v0, /device:TPU:0, one launch (start us, length us, event | category | flops | bytes accessed | tf_op | source)
XLA Modules:
  0.0 171.3 jit_solution(1325957787440588316)
XLA Ops:
  0.0 164.6 %image.1 = bf16[2,16,96,1024]{3,2,1,0:T(8,128)(2,1)} custom-call(bf16[2,16,256,384]{3,2,1,0:T(8,128)(2,1)} %polar.1, s32[256,384]{1,0:T(8,128)} %off_h.1, s32[256,384]{1,0:T(8,128)} %cnt_h.1, bf16[8,256,384]{2,1,0:T(8,128)(2,1)} %tap_h.1), custom_call_target="tpu_custom_call" | custom-call | tf_op jit(solution)/shard_map/image/pallas_call | solution.py:623
  164.6 6.6 %copy.6 = bf16[2,16,96,1024]{3,2,1,0:T(8,128)(2,1)} copy(bf16[2,16,96,1024]{3,2,1,0:T(8,128)(2,1)} %image.1) | data formatting | bytes 12582912
where the time goes:
time: 173 us; the launch traced here: 171 us
  Pallas kernels  165 us (95%)
  local copies, waits for them, and re-layouts  6.64 us (4%)
    pallas_call x1, Pallas kernels, fused(): pl.pallas_call(fused_body, out_shape=jax.ShapeDtypeStruct((2, heights, bi...  165 us
    unnamed x1, local copies, waits for them, and re-layouts  6.64 us

commit v1 on v0

--- a/solution.py
+++ b/solution.py
@@ -16,7 +16,10 @@
 GROUP = 16
 TAPS = 2 * HW + 1
 BATCH = 4
-LATE = 4
+LATE = 3
+EARLY = 3
+AHEAD = 10
+HALVES = 2
 SLOTS = 4
 FIRST = 2
 SPLIT = 2
@@ -203,9 +206,13 @@
             at_az(shift),
         )
 
-    def xe_copy(c):
+    def xe_copy(c, g):
         return remote(
-            er.at[:, :, 0, :, c], er.at[:, :, 1, :, c], xe_s.at[c], xe_r.at[c], el_peer
+            er.at[g, :, 0, :, c],
+            er.at[g, :, 1, :, c],
+            xe_s.at[c, g],
+            xe_r.at[c, g],
+            el_peer,
         )
 
     def ze_copy(g, q, shift, lanes):
@@ -224,14 +231,15 @@
             ch.at[:, 0, :, span], ch.at[:, 1, :, span], xa_s.at[b], xa_r.at[b], el_peer
         )
 
-    def xb_copy(b, g):
+    def xb_copy(b, g, k):
         span = pl.ds(b * BATCH, BATCH)
         half = batches // 2
+        lanes = pl.ds(k * (A // HALVES), A // HALVES)
         return remote(
-            ch.at[g, 0, :, span],
-            ch.at[g, 1, :, span],
-            xb_s.at[b - half, g],
-            xb_r.at[b - half, g],
+            ch.at[g, 0, :, span, :, lanes],
+            ch.at[g, 1, :, span, :, lanes],
+            xb_s.at[b - half, g, k],
+            xb_r.at[b - half, g, k],
             el_peer,
         )
 
@@ -396,15 +404,23 @@
                 for g in range(early_groups):
                     at = s * bins + late + g * GROUP
                     er[g, s, 0, p, c] = part[at : at + GROUP]
-        for s in order:
-            zl_copy(c, s, own_cols).start()
-        xe_copy(c).start()
-
-    middle = n_az // 2
-    order = [middle] + [s for s in range(1, n_az) if s != middle]
+        for core, shifts in enumerate((order[1:] + order[:1], order)):
+
+            @pl.when(fq == core)
+            def _():
+                for s in shifts:
+                    zl_copy(c, s, own_cols).start()
+
+        for g in range(early_groups - 1):
+            xe_copy(c, g).start()
+
+        @pl.when(c < AHEAD)
+        def _():
+            xe_copy(c, early_groups - 1).start()
+
+    order = list(range(1, n_az))
 
     def azimuth_tables():
-        size = 1024 // block
         col = iota((block, A), 1)
         lowc[...], lows[...] = small_trig(iota((block, A), 0) * col, A)
         highc[...], highs[...] = small_trig(iota((A // block, A), 0) * block * col, A)
@@ -471,6 +487,9 @@
                     ch[g, 0, p, span, :, lane_block(t, TILE)] = part[:, g]
 
     def early_heights(g):
+        for c in range(cuts):
+            xe_copy(c, g).wait_recv()
+
         @pl.loop(0, n_az)
         def _(s):
             data = er[g, s].reshape(4 * cuts * GROUP, cols)
@@ -516,16 +535,17 @@
             ost.at[g % 2], out_h.at[:, :, pl.ds(g * GROUP, GROUP), :], lo_sem.at[g]
         )
 
-    def late_heights(g):
-        if g == 0:
+    def late_heights(g, k):
+        if g == 0 and k == 0:
             for b in range(batches // 2):
                 xa_copy(b).wait_recv()
         for b in range(batches // 2, batches):
-            xb_copy(b, g).wait_recv()
-        if g >= 2:
+            xb_copy(b, g, k).wait_recv()
+        if g >= 2 and k == 0:
             late_out(g - 2).wait()
-
-        @pl.loop(0, A // TILE)
+        some = A // TILE // HALVES
+
+        @pl.loop(k * some, (k + 1) * some)
         def _(t):
             at = lane_block(t, TILE)
             data = ch[g, :, :, :, :, at].reshape(4 * cuts * GROUP, TILE)
@@ -533,7 +553,8 @@
             total = (total * (1.0 / math.sqrt(E))).astype(jnp.bfloat16)
             ost[g % 2, :, :, :, at] = total.reshape(2, heights, GROUP, TILE)
 
-        late_out(g).start()
+        if k == HALVES - 1:
+            late_out(g).start()
 
     def front(first, last):
         @pl.loop(first, last)
@@ -546,33 +567,36 @@
             def _():
                 range_step(c - 1)
 
-    pause = cuts // 2 + 2
-    front(0, pause)
+    front(0, cuts + 1)
+    for c in range(AHEAD, cuts):
+        xe_copy(c, early_groups - 1).start()
+    height_tables()
+    early_heights(0)
     azimuth_tables()
-    height_tables()
     cross_late(0)
     xa_copy(0).start()
-    front(pause, cuts + 1)
     cross_late(1)
     xa_copy(1).start()
-    cross_late(2)
-    xb_copy(2, 0).start()
-    xb_copy(2, 1).start()
-    for c in range(cuts):
-        xe_copy(c).wait_recv()
-    for g in range(early_groups):
+    for g in range(1, early_groups):
         early_heights(g)
-    cross_late(3)
-    for b, g in ((3, 0), (3, 1), (2, 2), (3, 2), (2, 3), (3, 3)):
-        xb_copy(b, g).start()
+    for b in range(batches // 2, batches):
+        cross_late(b)
+    for g in range(LATE):
+        for k in range(HALVES):
+            for b in range(batches // 2, batches):
+                xb_copy(b, g, k).start()
     cross_early(0, 0)
-    late_heights(0)
     cross_early(0, 1)
-    late_heights(1)
     cross_early(1, 0)
-    late_heights(2)
+    late_heights(0, 0)
+    late_heights(0, 1)
     cross_early(1, 1)
-    late_heights(3)
+    late_heights(1, 0)
+    late_heights(1, 1)
+    cross_early(2, 0)
+    late_heights(2, 0)
+    cross_early(2, 1)
+    late_heights(2, 1)
 
     @pl.when(az < n_az - 1)
     def _():
@@ -589,7 +613,8 @@
         fq_copy(c, lane_block(fq, freqs)).wait_send()
         for s in order:
             zl_copy(c, s, own_cols).wait_send()
-        xe_copy(c).wait_send()
+        for g in range(early_groups):
+            xe_copy(c, g).wait_send()
 
     for g in range(early_groups):
         for q in range(SPLIT):
@@ -599,7 +624,8 @@
         xa_copy(b).wait_send()
     for b in range(batches // 2, batches):
         for g in range(LATE):
-            xb_copy(b, g).wait_send()
+            for k in range(HALVES):
+                xb_copy(b, g, k).wait_send()
     for g in range(early_groups):
         for q in range(SPLIT):
             early_out(g, q).wait()
@@ -659,14 +685,14 @@
             dma((cuts,)),
             dma((cuts, far)),
             dma((cuts, far)),
-            dma((cuts,)),
-            dma((cuts,)),
+            dma((cuts, groups)),
+            dma((cuts, groups)),
             dma((groups, SPLIT, far)),
             dma((groups, SPLIT, far)),
             dma((batches // 2,)),
             dma((batches // 2,)),
-            dma((batches // 2, LATE)),
-            dma((batches // 2, LATE)),
+            dma((batches // 2, LATE, HALVES)),
+            dma((batches // 2, LATE, HALVES)),
             dma((LATE,)),
             dma((groups, SPLIT)),
         ],
@@ -686,7 +712,7 @@
         and lax.axis_size("el") == 2
         and az_count == 4
         and e_here == 4 * BATCH
-        and bins == (LATE + 2) * GROUP
+        and bins == (LATE + EARLY) * GROUP
         and col_count == TILE
         and freq_count % LANES == 0
     )

time: 173 us -> 161 us (0.931)
  Pallas kernels: 165 us -> 154 us
    pallas_call x1, Pallas kernels: 165 us -> 154 us  [fused(): pl.pallas_call(fused_body, out_shape=jax.ShapeDtypeStruct((2, heights, bi...]
where the time goes in v1:
time: 161 us
  Pallas kernels  154 us (96%)
  local copies, waits for them, and re-layouts  6.64 us (4%)
    pallas_call x1, Pallas kernels, fused(): pl.pallas_call(fused_body, out_shape=jax.ShapeDtypeStruct((2, heights, bi...  154 us
    unnamed x1, local copies, waits for them, and re-layouts  6.64 us

profile of v1, /device:TPU:0, one launch (start us, length us, event | category | flops | bytes accessed | tf_op | source)
XLA Modules:
  0.0 160.9 jit_solution(5714531794114583461)
XLA Ops:
  0.0 154.3 %image.1 = bf16[2,16,96,1024]{3,2,1,0:T(8,128)(2,1)} custom-call(bf16[2,16,256,384]{3,2,1,0:T(8,128)(2,1)} %polar.1, s32[256,384]{1,0:T(8,128)} %off_h.1, s32[256,384]{1,0:T(8,128)} %cnt_h.1, bf16[8,256,384]{2,1,0:T(8,128)(2,1)} %tap_h.1), custom_call_target="tpu_custom_call" | custom-call | tf_op jit(solution)/shard_map/image/pallas_call | solution.py:649
  154.3 6.6 %copy.6 = bf16[2,16,96,1024]{3,2,1,0:T(8,128)(2,1)} copy(bf16[2,16,96,1024]{3,2,1,0:T(8,128)(2,1)} %image.1) | data formatting | bytes 12582912

commit v2 on v1

--- a/solution.py
+++ b/solution.py
@@ -127,12 +127,12 @@
 
 
 def fused_body(
-    polar, off_h, cnt_h, tap_h, out_h,
+    polar, off_h, cnt_h, tap_h, out,
     xs, buf, pv, wt, offv, cntv, tapv, hl, hr,
     lowc, lows, highc, highs, rtab, cos_a, sin_a, htab,
-    rl, zl, er, eh, ez, ch, ost, est,
+    rl, zl, er, eh, ez, ch,
     in_sem, pv_sem, halo_s, halo_r, fq_s, fq_r, zl_s, zl_r,
-    xe_s, xe_r, ze_s, ze_r, xa_s, xa_r, xb_s, xb_r, lo_sem, eo_sem,
+    xe_s, xe_r, ze_s, ze_r, xa_s, xa_r, xb_s, xb_r,
 ):
     n_az = lax.axis_size("az")
     az, fq, el = (lax.axis_index(name) for name in ("az", "fq", "el"))
@@ -140,7 +140,7 @@
     parts = freqs // LANES
     heights = E // 2
     late = LATE * GROUP
-    bins = out_h.shape[2]
+    bins = out.shape[2]
     early_groups = (bins - late) // GROUP
     batches = cuts // BATCH
     steps = cols // GROUP
@@ -329,7 +329,7 @@
                 for d in range(size)
             ]
         for d in range(TAPS):
-            wt[d, g, rows, :] = taps[d]
+            wt[d, g, rows, :] = taps[d].astype(jnp.bfloat16)
 
     def wait_halo(k):
         @pl.when(az > 0)
@@ -364,7 +364,9 @@
             g = i // steps
             base = pl.multiple_of(lax.rem(i, steps) * GROUP, GROUP)
             lanes = lane_block(fq * parts + g, LANES)
-            weights = [wt[d, g, pl.ds(base, GROUP), :] for d in range(TAPS)]
+            weights = [
+                wt[d, g, pl.ds(base, GROUP), :].astype(jnp.float32) for d in range(TAPS)
+            ]
             for p in range(2):
                 acc = [None, None]
                 for o in range(TAPS + 8):
@@ -509,14 +511,6 @@
             for s in order:
                 ze_copy(g, q, s, own_cols).start()
 
-    def early_out(g, q):
-        span = pl.ds(q * (heights // SPLIT), heights // SPLIT)
-        return pltpu.make_async_copy(
-            est.at[g, q],
-            out_h.at[:, span, pl.ds(late + g * GROUP, GROUP), :],
-            eo_sem.at[g, q],
-        )
-
     def cross_early(g, q):
         for s in order:
             ze_copy(g, q, s, from_az(s)).wait_recv()
@@ -526,14 +520,10 @@
         def _(t):
             left = ez[g, :, q * some : (q + 1) * some].reshape(2 * some * GROUP, A)
             for p, part in enumerate(cross_tile(left, t)):
-                est[g, q, p, :, :, lane_block(t, TILE)] = part.reshape(some, GROUP, TILE)
-
-        early_out(g, q).start()
-
-    def late_out(g):
-        return pltpu.make_async_copy(
-            ost.at[g % 2], out_h.at[:, :, pl.ds(g * GROUP, GROUP), :], lo_sem.at[g]
-        )
+                at = late + g * GROUP
+                out[p, q * some : (q + 1) * some, at : at + GROUP, lane_block(t, TILE)] = (
+                    part.reshape(some, GROUP, TILE)
+                )
 
     def late_heights(g, k):
         if g == 0 and k == 0:
@@ -541,8 +531,6 @@
                 xa_copy(b).wait_recv()
         for b in range(batches // 2, batches):
             xb_copy(b, g, k).wait_recv()
-        if g >= 2 and k == 0:
-            late_out(g - 2).wait()
         some = A // TILE // HALVES
 
         @pl.loop(k * some, (k + 1) * some)
@@ -551,10 +539,7 @@
             data = ch[g, :, :, :, :, at].reshape(4 * cuts * GROUP, TILE)
             total = jnp.dot(htab[...], data, preferred_element_type=jnp.float32)
             total = (total * (1.0 / math.sqrt(E))).astype(jnp.bfloat16)
-            ost[g % 2, :, :, :, at] = total.reshape(2, heights, GROUP, TILE)
-
-        if k == HALVES - 1:
-            late_out(g).start()
+            out[:, :, g * GROUP : (g + 1) * GROUP, at] = total.reshape(2, heights, GROUP, TILE)
 
     def front(first, last):
         @pl.loop(first, last)
@@ -626,11 +611,6 @@
         for g in range(LATE):
             for k in range(HALVES):
                 xb_copy(b, g, k).wait_send()
-    for g in range(early_groups):
-        for q in range(SPLIT):
-            early_out(g, q).wait()
-    for g in range(LATE - 2, LATE):
-        late_out(g).wait()
 
 
 def fused(polar, band_offset, tap_count, tap_weight):
@@ -648,14 +628,14 @@
     dma = pltpu.SemaphoreType.DMA
     return pl.pallas_call(
         fused_body,
-        out_shape=jax.ShapeDtypeStruct((2, heights, bins, A), half),
+        out_shape=pltpu.VMEM((2, heights, bins, A), half),
         in_specs=[pl.BlockSpec(memory_space=pl.ANY)] * 4,
-        out_specs=pl.BlockSpec(memory_space=pl.ANY),
+        out_specs=pl.BlockSpec(memory_space=pltpu.VMEM),
         scratch_shapes=[
             vmem((cuts, 2, cols, F), half),
             vmem((2, parts, cols + 2 * HW, LANES), jnp.float32),
             vmem((SLOTS, 2, cols, freqs), half),
-            vmem((TAPS, parts, cols, LANES), jnp.float32),
+            vmem((TAPS, parts, cols, LANES), half),
             vmem((cols, freqs), jnp.int32),
             vmem((cols, freqs), jnp.int32),
             vmem((KT, cols, freqs), half),
@@ -675,8 +655,6 @@
             vmem((groups, far, 2, heights, GROUP, cols), half),
             vmem((groups, 2, heights, GROUP, A), half),
             vmem((LATE, 2, 2, cuts, GROUP, A), half),
-            vmem((2, 2, heights, GROUP, A), half),
-            vmem((groups, SPLIT, 2, heights // SPLIT, GROUP, A), half),
             dma((3,)),
             dma((SLOTS,)),
             dma((2, 2)),
@@ -693,11 +671,9 @@
             dma((batches // 2,)),
             dma((batches // 2, LATE, HALVES)),
             dma((batches // 2, LATE, HALVES)),
-            dma((LATE,)),
-            dma((groups, SPLIT)),
         ],
         compiler_params=pltpu.CompilerParams(
-            collective_id=0, has_side_effects=True, vmem_limit_bytes=67043328
+            collective_id=0, has_side_effects=True, vmem_limit_bytes=60000000
         ),
         name="image",
     )(polar, band_offset, tap_count, tap_weight)

time: 161 us -> 157 us (0.975)
  local copies, waits for them, and re-layouts: 6.64 us -> 2.71 us
    unnamed x1, local copies, waits for them, and re-layouts: 6.64 us -> 2.71 us
where the time goes in v2:
time: 157 us; the launch traced here: 156 us
  Pallas kernels  154 us (98%)
  local copies, waits for them, and re-layouts  2.71 us (2%)
    pallas_call x1, Pallas kernels, fused(): pl.pallas_call(fused_body, out_shape=pltpu.VMEM((2, heights, bins, A), ha...  154 us

profile of v2, /device:TPU:0, one launch (start us, length us, event | category | flops | bytes accessed | tf_op | source)
XLA Modules:
  0.0 156.4 jit_solution(9121138865601000124)
XLA Ops:
  0.0 153.6 %image.1 = bf16[2,16,96,1024]{3,2,1,0:T(8,128)(2,1)S(1)} custom-call(bf16[2,16,256,384]{3,2,1,0:T(8,128)(2,1)} %polar.1, s32[256,384]{1,0:T(8,128)} %off_h.1, s32[256,384]{1,0:T(8,128)} %cnt_h.1, bf16[8,256,384]{2,1,0:T(8,128)(2,1)} %tap_h.1), custom_call_target="tpu_custom_call" | custom-call | tf_op jit(solution)/shard_map/image/pallas_call | solution.py:629
  153.7 2.7 %copy.6 = bf16[2,16,96,1024]{3,2,1,0:T(8,128)(2,1)} copy(bf16[2,16,96,1024]{3,2,1,0:T(8,128)(2,1)S(1)} %image.1) | data formatting | bytes 12582912

commit v3 on v2

--- a/solution.py
+++ b/solution.py
@@ -19,7 +19,7 @@
 LATE = 3
 EARLY = 3
 AHEAD = 10
-HALVES = 2
+HALVES = 4
 SLOTS = 4
 FIRST = 2
 SPLIT = 2
@@ -343,26 +343,13 @@
     def interpolate(c):
         slot = lax.rem(c, SLOTS)
         polar_copy(c).wait()
-
-        @pl.when(c == 0)
-        def _():
-            wait_halo(0)
-
-        @pl.when(c == FIRST)
-        def _():
-            wait_halo(1)
-
         for p in range(2):
             for g in range(parts):
                 lanes = slice(g * LANES, (g + 1) * LANES)
-                buf[p, g, 0:HW, :] = hl[p, c, :, lanes].astype(jnp.float32)
                 buf[p, g, HW : HW + cols, :] = pv[slot, p, :, lanes].astype(jnp.float32)
-                buf[p, g, HW + cols :, :] = hr[p, c, :, lanes].astype(jnp.float32)
-
-        @pl.loop(0, parts * steps)
-        def _(i):
-            g = i // steps
-            base = pl.multiple_of(lax.rem(i, steps) * GROUP, GROUP)
+
+        def combine(g, r):
+            base = pl.multiple_of(r * GROUP, GROUP)
             lanes = lane_block(fq * parts + g, LANES)
             weights = [
                 wt[d, g, pl.ds(base, GROUP), :].astype(jnp.float32) for d in range(TAPS)
@@ -378,6 +365,30 @@
                             acc[v] = term if acc[v] is None else acc[v] + term
                 value = jnp.concatenate(acc, axis=0).astype(jnp.bfloat16)
                 xs[c, p, pl.ds(base, GROUP), lanes] = value
+
+        inside = steps - 2
+
+        @pl.loop(0, parts * inside)
+        def _(i):
+            combine(i // inside, 1 + lax.rem(i, inside))
+
+        @pl.when(c == 0)
+        def _():
+            wait_halo(0)
+
+        @pl.when(c == FIRST)
+        def _():
+            wait_halo(1)
+
+        for p in range(2):
+            for g in range(parts):
+                lanes = slice(g * LANES, (g + 1) * LANES)
+                buf[p, g, 0:HW, :] = hl[p, c, :, lanes].astype(jnp.float32)
+                buf[p, g, HW + cols :, :] = hr[p, c, :, lanes].astype(jnp.float32)
+
+        @pl.loop(0, parts * 2)
+        def _(i):
+            combine(i // 2, lax.rem(i, 2) * (steps - 1))
 
         fq_copy(c, lane_block(fq, freqs)).start()
 
@@ -555,11 +566,11 @@
     front(0, cuts + 1)
     for c in range(AHEAD, cuts):
         xe_copy(c, early_groups - 1).start()
-    height_tables()
-    early_heights(0)
     azimuth_tables()
     cross_late(0)
     xa_copy(0).start()
+    height_tables()
+    early_heights(0)
     cross_late(1)
     xa_copy(1).start()
     for g in range(1, early_groups):
@@ -573,15 +584,16 @@
     cross_early(0, 0)
     cross_early(0, 1)
     cross_early(1, 0)
-    late_heights(0, 0)
-    late_heights(0, 1)
+    for k in range(HALVES):
+        late_heights(0, k)
     cross_early(1, 1)
-    late_heights(1, 0)
-    late_heights(1, 1)
+    for k in range(HALVES):
+        late_heights(1, k)
     cross_early(2, 0)
-    late_heights(2, 0)
+    for k in range(HALVES - 1):
+        late_heights(2, k)
     cross_early(2, 1)
-    late_heights(2, 1)
+    late_heights(2, HALVES - 1)
 
     @pl.when(az < n_az - 1)
     def _():

time: 157 us -> 157 us (level)
  no operation moved by 1% of the time
where the time goes in v3:
time: 157 us
  Pallas kernels  154 us (98%)
  local copies, waits for them, and re-layouts  2.71 us (2%)
    pallas_call x1, Pallas kernels, fused(): pl.pallas_call(fused_body, out_shape=pltpu.VMEM((2, heights, bins, A), ha...  154 us

profile of v3, /device:TPU:0, one launch (start us, length us, event | category | flops | bytes accessed | tf_op | source)
XLA Modules:
  0.0 157.1 jit_solution(7574438876955095453)
XLA Ops:
  0.0 154.4 %image.1 = bf16[2,16,96,1024]{3,2,1,0:T(8,128)(2,1)S(1)} custom-call(bf16[2,16,256,384]{3,2,1,0:T(8,128)(2,1)} %polar.1, s32[256,384]{1,0:T(8,128)} %off_h.1, s32[256,384]{1,0:T(8,128)} %cnt_h.1, bf16[8,256,384]{2,1,0:T(8,128)(2,1)} %tap_h.1), custom_call_target="tpu_custom_call" | custom-call | tf_op jit(solution)/shard_map/image/pallas_call | solution.py:641
  154.4 2.7 %copy.6 = bf16[2,16,96,1024]{3,2,1,0:T(8,128)(2,1)} copy(bf16[2,16,96,1024]{3,2,1,0:T(8,128)(2,1)S(1)} %image.1) | data formatting | bytes 12582912

commit v4 on v2

--- a/solution.py
+++ b/solution.py
@@ -208,8 +208,8 @@
 
     def xe_copy(c, g):
         return remote(
-            er.at[g, :, 0, :, c],
-            er.at[g, :, 1, :, c],
+            er.at[g, 0, c],
+            er.at[g, 1, c],
             xe_s.at[c, g],
             xe_r.at[c, g],
             el_peer,
@@ -228,7 +228,7 @@
     def xa_copy(b):
         span = pl.ds(b * BATCH, BATCH)
         return remote(
-            ch.at[:, 0, :, span], ch.at[:, 1, :, span], xa_s.at[b], xa_r.at[b], el_peer
+            ch.at[:, 0, span], ch.at[:, 1, span], xa_s.at[b], xa_r.at[b], el_peer
         )
 
     def xb_copy(b, g, k):
@@ -236,8 +236,8 @@
         half = batches // 2
         lanes = pl.ds(k * (A // HALVES), A // HALVES)
         return remote(
-            ch.at[g, 0, :, span, :, lanes],
-            ch.at[g, 1, :, span, :, lanes],
+            ch.at[g, 0, span, :, :, lanes],
+            ch.at[g, 1, span, :, :, lanes],
             xb_s.at[b - half, g, k],
             xb_r.at[b - half, g, k],
             el_peer,
@@ -405,7 +405,7 @@
                     rl[c, s - 1, p] = piece
                 for g in range(early_groups):
                     at = s * bins + late + g * GROUP
-                    er[g, s, 0, p, c] = part[at : at + GROUP]
+                    er[g, 0, c, p, s] = part[at : at + GROUP]
         for core, shifts in enumerate((order[1:] + order[:1], order)):
 
             @pl.when(fq == core)
@@ -441,9 +441,9 @@
         height = el * heights + jnp.where(out_imag, row - heights, row)
         other = col >= 2 * cuts
         inner = jnp.where(other, col - 2 * cuts, col)
-        in_imag = inner >= cuts
+        in_imag = (inner & 1) == 1
         source = jnp.where(other, 1 - el, el)
-        elev = source * cuts + jnp.where(in_imag, inner - cuts, inner)
+        elev = source * cuts + (inner >> 1)
         cos_e, sin_e = small_trig(height * elev, E)
         sign = jnp.where(out_imag, sin_e, -sin_e)
         small = jnp.where(out_imag == in_imag, cos_e, sign)
@@ -486,7 +486,7 @@
                 part = part.reshape(BATCH, LATE, GROUP, TILE)
                 for g in range(LATE):
                     span = pl.ds(b * BATCH, BATCH)
-                    ch[g, 0, p, span, :, lane_block(t, TILE)] = part[:, g]
+                    ch[g, 0, span, p, :, lane_block(t, TILE)] = part[:, g]
 
     def early_heights(g):
         for c in range(cuts):
@@ -494,7 +494,7 @@
 
         @pl.loop(0, n_az)
         def _(s):
-            data = er[g, s].reshape(4 * cuts * GROUP, cols)
+            data = er[g, :, :, :, s].reshape(4 * cuts * GROUP, cols)
             total = jnp.dot(htab[...], data, preferred_element_type=jnp.float32)
             total = (total * (1.0 / math.sqrt(E))).astype(jnp.bfloat16)
             total = total.reshape(2, heights, GROUP, cols)
@@ -651,10 +651,10 @@
             vmem((2 * heights * GROUP, 4 * cuts * GROUP), half),
             vmem((cuts, far, 2, late, cols), half),
             vmem((batches, 2, BATCH, late, A), half),
-            vmem((groups, n_az, 2, 2, cuts, GROUP, cols), half),
+            vmem((groups, 2, cuts, 2, n_az, GROUP, cols), half),
             vmem((groups, far, 2, heights, GROUP, cols), half),
             vmem((groups, 2, heights, GROUP, A), half),
-            vmem((LATE, 2, 2, cuts, GROUP, A), half),
+            vmem((LATE, 2, cuts, 2, GROUP, A), half),
             dma((3,)),
             dma((SLOTS,)),
             dma((2, 2)),

time: 157 us -> 157 us (level)
  no operation moved by 1% of the time
where the time goes in v4:
time: 157 us; the launch traced here: 156 us
  Pallas kernels  154 us (98%)
  local copies, waits for them, and re-layouts  2.71 us (2%)
    pallas_call x1, Pallas kernels, fused(): pl.pallas_call(fused_body, out_shape=pltpu.VMEM((2, heights, bins, A), ha...  154 us

profile of v4, /device:TPU:0, one launch (start us, length us, event | category | flops | bytes accessed | tf_op | source)
XLA Modules:
  0.0 156.4 jit_solution(8129738333069450139)
XLA Ops:
  0.0 153.6 %image.1 = bf16[2,16,96,1024]{3,2,1,0:T(8,128)(2,1)S(1)} custom-call(bf16[2,16,256,384]{3,2,1,0:T(8,128)(2,1)} %polar.1, s32[256,384]{1,0:T(8,128)} %off_h.1, s32[256,384]{1,0:T(8,128)} %cnt_h.1, bf16[8,256,384]{2,1,0:T(8,128)(2,1)} %tap_h.1), custom_call_target="tpu_custom_call" | custom-call | tf_op jit(solution)/shard_map/image/pallas_call | solution.py:629
  153.7 2.7 %copy.6 = bf16[2,16,96,1024]{3,2,1,0:T(8,128)(2,1)} copy(bf16[2,16,96,1024]{3,2,1,0:T(8,128)(2,1)S(1)} %image.1) | data formatting | bytes 12582912
